TPU v7x, 32 devices: a whole 2x2x4 slice. The times are simulated.
32 devices in a mesh: gx: 8 (over y, x, core), gy: 4 (over z).
Axes of the slice: x: 2, y: 2, z: 4, core: 2. Of those that a mesh axis runs over, the one named last changes fastest.
Arguments:
- tracers: float32 [96, 256, 2, 128], P('gx', 'gy'), may hold values from -6 to 6
- weights: float32 [96, 256, 48], P('gx', 'gy'), may hold values from 0 to 0.5
- offsets: int32 [96, 256, 4], P('gx', 'gy'), may hold values from -2 to 1
- owner: int32 [2, 8], replicated, may hold values from 0 to 7, as said below
- codes: int32 [2, 8], replicated, may hold values from 0 to 3
Outputs:
- updated: float32 [96, 256, 2, 128], P('gx', 'gy')
Inputs may be any that keep to these rules, and one draw needn't show every extreme that they name: owner[0, b] names the column block whose first three rows are glued below block b, owner[1, b] the one whose last three rows are glued above it; each row of owner is a permutation of the 8 blocks, so every block's edge rows are glued to exactly one block on each side. `codes`: bit 0 reverses the glued rows along the columns, bit 1 reverses their order.
All inputs are finite; a program needn't handle non-finite values.
Results may differ from a plain program's by a relative error of at most 0.0003.
Values sent between devices are 32-bit elements; how exact they have to be, the bound alone decides.
No kernel may reach another device: no remote copies, remote signals or barrier semaphores. Data moves between devices by JAX's collectives and lax.ppermute only.
A program may use at most 128 MiB of HBM per device.

v0:
```python
import functools

import jax
import jax.numpy as jnp
import numpy as np
from jax import lax
from jax.experimental import pallas as pl
from jax.experimental.pallas import tpu as pltpu
from jax.sharding import PartitionSpec as P

HALO = 3
BLOCK_X = 4
BLOCK_Y = 16
PITCH = 24
LANES = 128
LEAD = 4
BF16 = jnp.bfloat16
F32 = jnp.float32

STENCILS = [
    {(0, 0): 1.0},
    {(1, 0): 0.5, (-1, 0): -0.5},
    {(0, 1): 0.5, (0, -1): -0.5},
    {(1, 0): 0.5, (0, 0): -1.0, (-1, 0): 0.5},
    {(0, 1): 0.5, (0, 0): -1.0, (0, -1): 0.5},
    {(1, 1): 0.25, (1, -1): -0.25, (-1, 1): -0.25, (-1, -1): 0.25},
]


def spread_matrix(levels):
    terms = 24 * levels
    rows = 2 * terms + 8 * pl.cdiv(2 * levels, 8)
    matrix = np.zeros((rows, 2 * levels * LANES), np.float32)
    for level in range(levels):
        for piece in range(4):
            for moment, stencil in enumerate(STENCILS):
                for (east, north), value in stencil.items():
                    lane = (piece // 2 + 1 + east) * PITCH + piece % 2 + 1 + north
                    row = 24 * level + 6 * piece + moment
                    matrix[row, level * LANES + lane] += value
                    matrix[terms + row, level * LANES + lane] += value
        first = (levels + level) * LANES
        matrix[2 * terms + 2 * level, first : first + LANES] = PITCH
        matrix[2 * terms + 2 * level + 1, first : first + LANES] = 1
    return matrix


def load_kernel(count, ends, run, turns, owner_ref, codes_ref, cells_ref, weights_ref, offsets_ref,
                matrix_ref, after_ref, *refs):
    del after_ref
    table_ref, inner_ref, weights_out, offsets_out, matrix_out, field_ref, owner, codes, sems = refs[-9:]

    @pl.when(((lax.axis_index("gx") + 1) // 2 % 2 == 0) == turns)
    def _():
        index, place = lax.axis_index("gx"), lax.axis_index("gy")
        cols, rows, _ = cells_ref.shape
        lead = LEAD * (weights_ref.shape[1] // 24)
        last = cols - HALO
        pairs = [
            (owner_ref, owner),
            (codes_ref, codes),
            (cells_ref.at[pl.ds(jnp.where(index % 2 == 0, last, 0), HALO)], inner_ref),
            (weights_ref, weights_out),
            (offsets_ref, offsets_out),
            (matrix_ref, matrix_out),
        ]
        for col in range(0, cols, BLOCK_X):
            to = field_ref.at[pl.ds(HALO + col, BLOCK_X), pl.ds(lead, rows)]
            pairs.append((cells_ref.at[pl.ds(col, BLOCK_X)], to))
        copies = [pltpu.make_async_copy(a, b, sems.at[at]) for at, (a, b) in enumerate(pairs)]
        for copy in copies:
            copy.start()
        copies[0].wait()
        copies[1].wait()
        side = jnp.where(place == 0, 0, 1)
        window = Window(cells_ref.shape[0], 0, count, run, None)
        target = lax.rem(index + count // 2, count)
        is_end = jnp.logical_or(place == 0, place == ends - 1)
        code = jnp.where(is_end, codes[side, index], 0)
        lines = [window.start(owner[side, target]), window.start(owner[side, index]), code]
        for at, line in enumerate(lines):
            table_ref[at : at + 1] = jnp.full((1, LANES), line, jnp.int32)
        for copy in copies[2:]:
            copy.wait()


def band_kernel(levels, rows, block, weights_ref, offsets_ref, matrix_ref, after_ref, band_ref):
    del after_ref
    y_blocks = rows // BLOCK_Y
    lane = lax.broadcasted_iota(jnp.int32, (rows, LANES), 1)
    row_in = lax.broadcasted_iota(jnp.int32, (rows, LANES), 0) % BLOCK_Y
    base = lane - row_in - 2 * PITCH - 2
    pad = matrix_ref.shape[0] - 2 * weights_ref.shape[1] - offsets_ref.shape[1]

    def column(x):
        weights = weights_ref[x]
        high = weights.astype(BF16).astype(F32)
        stacked = jnp.concatenate(
            [high, weights - high, offsets_ref[x].astype(F32), jnp.zeros((pad, rows), F32)], axis=0
        ).astype(BF16)
        spread = lax.dot_general(
            stacked, matrix_ref[...], (((0,), (0,)), ((), ())), preferred_element_type=F32
        )
        inner = x % BLOCK_X
        at = inner * BLOCK_Y
        low = at + BLOCK_X * BLOCK_Y
        for level in range(levels):
            points = spread[:, level * LANES : (level + 1) * LANES]
            first = (levels + level) * LANES
            shift = spread[:, first : first + LANES].astype(jnp.int32)
            for y in range(y_blocks):
                mine = slice(y * BLOCK_Y, (y + 1) * BLOCK_Y)
                index = base[mine] - shift[mine] - inner * PITCH
                picked = jnp.take_along_axis(
                    points[mine], index & (LANES - 1), axis=1, mode="promise_in_bounds"
                )
                top = picked.astype(BF16).astype(F32)
                rest = picked - top
                here = index >= 0
                slot = y * levels + level
                for part in range(2):
                    lanes = slice(part * LANES, (part + 1) * LANES)
                    keep = here if part == 0 else jnp.logical_not(here)
                    band_ref[slot, at : at + BLOCK_Y, lanes] = jnp.where(keep, top, 0.0).astype(BF16)
                    band_ref[slot, low : low + BLOCK_Y, lanes] = jnp.where(keep, rest, 0.0).astype(BF16)

    for step in range(BLOCK_X):
        column(block * BLOCK_X + step)


def pack_kernel(ends, cells_ref, edges_ref, message_ref, outer_ref, low_ref, high_ref, sems):
    cols, rows, _ = cells_ref.shape
    width = edges_ref.shape[0] // cols // 2
    deep = low_ref.shape[1]
    even, place = lax.axis_index("gx") % 2 == 0, lax.axis_index("gy")
    low, up = place == 0, place % 2 == 0
    is_end = jnp.logical_or(low, place == ends - 1)
    last = cols - HALO
    copies = [
        pltpu.make_async_copy(cells_ref.at[:, pl.ds(0, deep)], low_ref, sems.at[0]),
        pltpu.make_async_copy(cells_ref.at[:, pl.ds(rows - deep, deep)], high_ref, sems.at[1]),
        pltpu.make_async_copy(
            cells_ref.at[pl.ds(jnp.where(even, 0, last), HALO)], outer_ref, sems.at[2]
        ),
    ]
    for copy in copies:
        copy.start()
    for copy in copies[:2]:
        copy.wait()
    for col in range(cols):
        at = 2 * width * col
        bottom, top = low_ref[col, :width], high_ref[col, deep - width :]
        edges_ref[at : at + width] = bottom
        edges_ref[at + width : at + 2 * width] = top
        strip = jnp.where(low, bottom, top)
        if col < HALO:
            bottom = jnp.where(even, bottom, low_ref[last + col, :width])
            top = jnp.where(even, top, high_ref[last + col, deep - width :])
            message_ref[width * col : width * (col + 1)] = jnp.where(up, top, bottom)
            strip = jnp.where(is_end, strip, jnp.where(up, bottom, top))
        to = width * (HALO + col)
        message_ref[to : to + width] = strip
    clear(message_ref, width * (HALO + cols))
    copies[2].wait()


def clear(ref, at):
    if at < ref.shape[0]:
        ref[at:] = jnp.zeros((ref.shape[0] - at, LANES), F32)


def relay_kernel(cols, width, ends, edges_ref, message_ref, got_ref, after_ref, relay_ref,
                 first_ref):
    del after_ref
    even, place = lax.axis_index("gx") % 2 == 0, lax.axis_index("gy")
    up = place % 2 == 0
    is_end = jnp.logical_or(place == 0, place == ends - 1)
    corner, strip = width * HALO, width * cols
    relay_ref[:strip] = message_ref[corner : corner + strip]
    relay_ref[strip : 2 * strip] = got_ref[corner : corner + strip]
    for col in range(HALO):
        left, right = 2 * width * col, 2 * width * (cols - HALO + col)
        low = jnp.where(even, edges_ref[right : right + width], edges_ref[left : left + width])
        left, right = left + width, right + width
        high = jnp.where(even, edges_ref[right : right + width], edges_ref[left : left + width])
        to = slice(width * col, width * (col + 1))
        relay_ref[to] = jnp.where(is_end, relay_ref[to], jnp.where(up, low, high))
    clear(relay_ref, 2 * strip)
    first_ref[:corner] = got_ref[:corner]
    for col in range(cols):
        at = 2 * width * col
        to = corner + width * col
        first_ref[to : to + width] = jnp.where(
            up, edges_ref[at + width : at + 2 * width], edges_ref[at : at + width]
        )
    clear(first_ref, corner + strip)


def turn_kernel(levels, cols, width, count, ends, run, first_ref, *refs):
    run_ref, table_ref, corner_ref, glued_ref, mask_ref = refs[-5:]
    even, place = lax.axis_index("gx") % 2 == 0, lax.axis_index("gy")
    size = HALO * width
    last = (HALO + cols) * width
    corner_ref[:size] = jnp.where(even, first_ref[last - size : last], first_ref[size : 2 * size])
    clear(corner_ref, size)
    wide = cols + 2 * HALO
    window = Window(cols, width, count, run, run_ref)
    start, code = table_ref[1:2, 0:1][0, 0], table_ref[2:3, 0:1][0, 0]
    is_end = jnp.logical_or(place == 0, place == ends - 1)
    mirrored, flipped = code % 2 == 1, code // 2 % 2 == 1
    for u in range(wide):
        to = slice(width * u, width * (u + 1))
        held, strip = window.column(start, jnp.where(mirrored, wide - 1 - u, u))
        glued_ref[to] = jnp.where(flipped, turn_rows(strip, levels), strip)
        mask_ref[to] = jnp.full(
            (width, LANES), jnp.where(jnp.logical_and(is_end, held), 1.0, 0.0), F32
        )
    clear(glued_ref, wide * width)
    clear(mask_ref, wide * width)


def turn_rows(strip, levels):
    return jnp.concatenate(
        [strip[levels * r : levels * (r + 1)] for r in reversed(range(HALO))], axis=0
    )


def join_kernel(cols, width, message_ref, got_ref, other_ref, after_ref, run_ref):
    del after_ref
    even = lax.axis_index("gx") % 2 == 0
    corner, strip = width * HALO, width * cols
    mine, far = message_ref[corner : corner + strip], got_ref[corner : corner + strip]
    near, beyond = other_ref[:strip], other_ref[strip : 2 * strip]
    pairs = ((far, beyond), (mine, near), (near, mine), (beyond, far))
    for at, (a, b) in enumerate(pairs):
        run_ref[at * strip : (at + 1) * strip] = jnp.where(even, a, b)


class Window:
    def __init__(self, cols, width, count, run, held):
        self.cols, self.width, self.total, self.run = cols, width, count * cols, run
        self.held = held
        index = lax.axis_index("gx")
        self.first = index - index % 2 - 1

    def start(self, owner):
        return lax.rem((owner - self.first) * self.cols - HALO + 2 * self.total, self.total)

    def column(self, start, step):
        at = start + step
        at = jnp.where(at >= self.total, at - self.total, at)
        row = jnp.minimum(at, self.run * self.cols - 1) * self.width
        return at < self.run * self.cols, self.held[pl.ds(row, self.width)]


def rows_kernel(cols, width, count, ends, run, table_ref, edges_ref, other_ref, got_ref, run_ref,
                second_ref):
    even, place = lax.axis_index("gx") % 2 == 0, lax.axis_index("gy")
    top = place % 2 == 1

    def column(u):
        if HALO <= u < HALO + cols:
            at = 2 * width * (u - HALO)
            return jnp.where(
                top, edges_ref[at + width : at + 2 * width], edges_ref[at : at + width]
            )
        col = u if u < HALO else u - HALO - cols
        near = other_ref[width * col : width * (col + 1)]
        far = got_ref[width * (HALO + col) : width * (HALO + col + 1)]
        return jnp.where(even == (u < HALO), far, near)

    wide = cols + 2 * HALO
    window = Window(cols, width, count, run, run_ref)
    start = table_ref[0:1, 0:1][0, 0]
    is_end = jnp.logical_or(place == 0, place == ends - 1)
    for u in range(wide):
        to = slice(u * width, (u + 1) * width)
        _, glued = window.column(start, u)
        second_ref[to] = jnp.where(is_end, glued, column(u))
    clear(second_ref, wide * width)


def block_sum(field_ref, bands, x, y, levels, level):
    size = BLOCK_X * BLOCK_Y
    reach = BLOCK_X + 2 * HALO
    begin = (y * BLOCK_Y + LEAD - HALO) * levels + level
    points = jnp.concatenate(
        [
            field_ref[x * BLOCK_X + c, pl.ds(begin, PITCH, stride=levels), :]
            for c in range(reach)
        ]
        + [jnp.zeros((2 * LANES - reach * PITCH, LANES), F32)],
        axis=0,
    )
    top = points.astype(BF16)
    rest = (points - top.astype(F32)).astype(BF16)
    band = bands[x][y * levels + level]
    product = jnp.dot(band, jnp.concatenate([top, rest], axis=1), preferred_element_type=F32)
    return product[:size, :LANES] + (product[:size, LANES:] + product[size:, :LANES])


def remap_blocks(field_ref, bands, stage_ref, levels, blocks, ready=None):
    for at, (x, y) in enumerate(blocks):
        for level in range(levels):
            total = block_sum(field_ref, bands, x, y, levels, level)
            for c in range(BLOCK_X):
                stage_ref[at, c, pl.ds(level, BLOCK_Y, stride=levels), :] = total[
                    c * BLOCK_Y : (c + 1) * BLOCK_Y
                ]
        if ready is not None:
            ready(at, x, y)


def middle_kernel(levels, blocks, inner_ref, outer_ref, after_ref, field_in, *refs):
    del after_ref, field_in
    *bands, field_ref, stage_ref = refs
    rows, wide = inner_ref.shape[1], field_ref.shape[0]
    lead = LEAD * levels
    even = lax.axis_index("gx") % 2 == 0
    for col in range(HALO):
        inner, outer = inner_ref[col], outer_ref[col]
        field_ref[col, lead : lead + rows] = jnp.where(even, outer, inner)
        field_ref[wide - HALO + col, lead : lead + rows] = jnp.where(even, inner, outer)
    remap_blocks(field_ref, bands, stage_ref, levels, blocks)


def put_block(source, out_ref, sem, x, y):
    _, deep, _ = source.shape
    to = out_ref.at[pl.ds(x * BLOCK_X, BLOCK_X), pl.ds(pl.multiple_of(y * deep, deep), deep)]
    copy = pltpu.make_async_copy(source, to, sem)
    copy.start()
    return copy


def near_kernel(levels, cols, rows, first_ref, corner_ref, field_in, *refs):
    del field_in
    *bands, field_ref, stage_ref = refs
    width, lead = HALO * levels, LEAD * levels
    even, up = lax.axis_index("gx") % 2 == 0, lax.axis_index("gy") % 2 == 0
    tail = field_ref.shape[1] - lead - rows - width
    for u in range(cols + 2 * HALO):
        if HALO <= u < HALO + cols:
            strip = first_ref[u * width : (u + 1) * width]
        else:
            col = u if u < HALO else u - HALO - cols
            far = first_ref[col * width : (col + 1) * width]
            near = corner_ref[col * width : (col + 1) * width]
            strip = jnp.where(even == (u < HALO), far, near)
        field_ref[u, lead - width : lead] = strip
        field_ref[u, lead + rows : lead + rows + width] = strip
        field_ref[u, lead + rows + width :] = jnp.zeros((tail, LANES), F32)
    last = rows // levels // BLOCK_Y - 1
    blocks = [(x, jnp.where(up, last, 0)) for x in range(cols // BLOCK_X)]
    remap_blocks(field_ref, bands, stage_ref, levels, blocks)


def edge_kernel(levels, cols, rows, done, table_ref, second_ref, glued_ref, mask_ref, near_ref,
                done_ref, field_in, *refs):
    del field_in
    *bands, field_ref, out_ref, stage_ref, sems = refs
    last = rows // levels // BLOCK_Y - 1
    up = lax.axis_index("gy") % 2 == 0
    blocks = [(x, jnp.where(up, 0, last)) for x in range(cols // BLOCK_X)]
    copies = []
    ready = [(done_ref.at[at], x, y) for at, (x, y) in enumerate(done)]
    ready += [(near_ref.at[x], x, last - y) for x, y in blocks]
    for source, x, y in ready:
        copies.append(put_block(source, out_ref, sems.at[len(copies)], x, y))

    def put(at, x, y):
        copies.append(put_block(stage_ref.at[at], out_ref, sems.at[len(copies)], x, y))

    width, lead = HALO * levels, LEAD * levels
    wide = cols + 2 * HALO
    code = table_ref[2:3, 0:1][0, 0]
    mirrored, flipped = code % 2 == 1, code // 2 % 2 == 1
    for u in range(wide):
        to = slice(width * u, width * (u + 1))
        back = slice(width * (wide - 1 - u), width * (wide - u))
        come = jnp.where(mirrored, second_ref[back], second_ref[to])
        come = jnp.where(flipped, turn_rows(come, levels), come)
        strip = jnp.where(mask_ref[to] > 0, glued_ref[to], come)
        for at, mine in ((lead - width, up), (lead + rows, jnp.logical_not(up))):
            old = field_ref[u, at : at + width]
            field_ref[u, at : at + width] = jnp.where(mine, strip, old)
    remap_blocks(field_ref, bands, stage_ref, levels, blocks, put)
    for copy in copies:
        copy.wait()


def grant(mebibytes):
    return pltpu.CompilerParams(vmem_limit_bytes=mebibytes << 20)


def takes(microseconds):
    return pl.CostEstimate(
        flops=0, bytes_accessed=int(microseconds * 3_000_000), transcendentals=0
    )


def in_hbm(array):
    return pltpu.with_memory_space_constraint(array, pltpu.HBM)


VMEM = pl.BlockSpec(memory_space=pltpu.VMEM)
HBM = pl.BlockSpec(memory_space=pltpu.HBM)
ANY = pl.BlockSpec(memory_space=pl.ANY)
SMEM = pl.BlockSpec(memory_space=pltpu.SMEM)


def shaped(*shape, dtype=F32):
    return jax.ShapeDtypeStruct(shape, dtype)


def eights(rows):
    return 8 * pl.cdiv(rows, 8)


def on_device(tracers, weights, offsets, owner, codes, matrix):
    cols, rows, levels, lanes = tracers.shape
    width = HALO * levels
    count, ends = lax.axis_size("gx"), lax.axis_size("gy")
    axes = ("gx", "gy")
    cells = tracers.reshape(cols, rows * levels, lanes)
    partner = [(i, i ^ 1) for i in range(count)]
    across = [(i, (i + 1) % count if i % 2 else (i - 1) % count) for i in range(count)]
    first_swap = [(i * ends + j, i * ends + (j ^ 1)) for i in range(count) for j in range(ends)]
    second_swap = []
    for i in range(count):
        for j in range(ends):
            if j in (0, ends - 1):
                second_swap.append((i * ends + j, (i + count // 2) % count * ends + j))
            else:
                second_swap.append((i * ends + j, i * ends + (j + 1 if j % 2 else j - 1)))

    deep = eights(width)
    strip, corner = width * cols, width * HALO
    columns = shaped(HALO, rows * levels, lanes)
    edges, message, outer = pl.pallas_call(
        functools.partial(pack_kernel, ends),
        out_shape=(shaped(2 * strip, lanes), shaped(eights(strip + corner), lanes), columns),
        in_specs=[HBM],
        out_specs=(VMEM, VMEM, VMEM),
        scratch_shapes=[
            pltpu.VMEM((cols, deep, lanes), F32),
            pltpu.VMEM((cols, deep, lanes), F32),
            pltpu.SemaphoreType.DMA((3,)),
        ],
        name="pack",
        compiler_params=grant(4),
        cost_estimate=takes(1.0),
    )(in_hbm(cells))
    got = lax.ppermute(message, "gx", across)
    outer_got = lax.ppermute(outer, "gx", across)

    field_rows = eights((LEAD + rows + HALO + PITCH - BLOCK_Y - 2 * HALO) * levels)
    field_shape = shaped(cols + 2 * HALO, field_rows, lanes)
    run = 4
    held = max(run, count // 2)
    weights = jnp.swapaxes(weights, 1, 2)
    offsets = jnp.swapaxes(offsets, 1, 2)
    loaded = (
        shaped(8, lanes, dtype=jnp.int32),
        columns,
        shaped(*weights.shape),
        shaped(*offsets.shape, dtype=jnp.int32),
        shaped(*matrix.shape, dtype=BF16),
        field_shape,
    )
    sources = [in_hbm(a) for a in (owner, codes, cells, weights, offsets, matrix)] + [message]

    def load(turns, into):
        return pl.pallas_call(
            functools.partial(load_kernel, count, ends, held, turns),
            out_shape=loaded,
            in_specs=[HBM] * 6 + [ANY] + [VMEM] * len(into),
            out_specs=(VMEM,) * 6,
            scratch_shapes=[
                pltpu.SMEM(owner.shape, jnp.int32),
                pltpu.SMEM(codes.shape, jnp.int32),
                pltpu.SemaphoreType.DMA((6 + cols // BLOCK_X,)),
            ],
            input_output_aliases={7 + at: at for at in range(len(into))},
            name="load",
            compiler_params=grant(6),
            cost_estimate=takes(0.5),
        )(*sources, *into)

    parts = load(False, ())
    table, inner, weights, offsets, matrix, field = load(True, parts)

    x_blocks, y_blocks = cols // BLOCK_X, rows // BLOCK_Y

    def band_of(block, after):
        return pl.pallas_call(
            functools.partial(band_kernel, levels, rows, block),
            out_shape=shaped(y_blocks * levels, 2 * BLOCK_X * BLOCK_Y, 2 * LANES, dtype=BF16),
            in_specs=[VMEM] * 3 + [ANY],
            out_specs=VMEM,
            name="band",
            compiler_params=grant(4),
            cost_estimate=takes(0.5),
        )(weights, offsets, matrix, after)

    relay, first = pl.pallas_call(
        functools.partial(relay_kernel, cols, width, ends),
        out_shape=(
            shaped(eights(2 * strip), lanes),
            shaped(eights(width * (cols + HALO)), lanes),
        ),
        in_specs=[VMEM] * 3 + [ANY],
        out_specs=(VMEM, VMEM),
        name="relay",
        compiler_params=grant(2),
        cost_estimate=takes(0.5),
    )(edges, message, got, table)
    other = lax.ppermute(relay, "gx", partner)
    first_got = lax.ppermute(first, axes, first_swap)
    inner_got = lax.ppermute(inner, "gx", partner)

    ring = pl.pallas_call(
        functools.partial(join_kernel, cols, width),
        out_shape=shaped(run * strip, lanes),
        in_specs=[VMEM] * 3 + [ANY],
        out_specs=VMEM,
        name="join",
        compiler_params=grant(2),
        cost_estimate=takes(0.5),
    )(message, got, other, relay)
    while run < held:
        shift = run
        more = lax.ppermute(ring, "gx", [((i + shift) % count, i) for i in range(count)])
        ring = jnp.concatenate([ring, more])
        run *= 2

    z_rows = eights(width * (cols + 2 * HALO))
    second = pl.pallas_call(
        functools.partial(rows_kernel, cols, width, count, ends, run),
        out_shape=shaped(z_rows, lanes),
        in_specs=[VMEM] * 5,
        out_specs=VMEM,
        name="rows",
        cost_estimate=takes(1.0),
        compiler_params=grant(2 * pl.cdiv(run, 8)),
    )(table, edges, other, got, ring)
    second_got = lax.ppermute(second, axes, second_swap)

    bands = [band_of(block, second) for block in range(x_blocks)]

    turned, glued, mask = pl.pallas_call(
        functools.partial(turn_kernel, levels, cols, width, count, ends, run),
        out_shape=(shaped(eights(width * HALO), lanes), shaped(z_rows, lanes), shaped(z_rows, lanes)),
        in_specs=[VMEM] + [ANY] * len(bands[:1]) + [VMEM] * 2,
        out_specs=(VMEM, VMEM, VMEM),
        name="turn",
        compiler_params=grant(2),
        cost_estimate=takes(0.1),
    )(first_got, *bands[:1], ring, table)
    turned_got = lax.ppermute(turned, "gx", partner)
    inside = [(x, y) for y in range(1, y_blocks - 1) for x in range(x_blocks)]
    block_shape = (BLOCK_X, BLOCK_Y * levels, lanes)
    middle = pl.pallas_call(
        functools.partial(middle_kernel, levels, inside),
        out_shape=(field_shape, shaped(len(inside), *block_shape)),
        in_specs=[VMEM, VMEM, ANY] + [VMEM] * (1 + x_blocks),
        out_specs=(VMEM, VMEM),
        input_output_aliases={3: 0},
        name="middle",
        cost_estimate=takes(0.7),
        compiler_params=grant(6),
    )
    field, done = middle(inner_got, outer_got, second, field, *bands)
    out_shape = shaped(cols, rows * levels, lanes)
    field, near = pl.pallas_call(
        functools.partial(near_kernel, levels, cols, rows * levels),
        out_shape=(field_shape, shaped(x_blocks, *block_shape)),
        in_specs=[VMEM] * (3 + x_blocks),
        out_specs=(VMEM, VMEM),
        input_output_aliases={2: 0},
        name="near",
        cost_estimate=takes(0.5),
        compiler_params=grant(6),
    )(first_got, turned_got, field, *bands)
    _, updated = pl.pallas_call(
        functools.partial(edge_kernel, levels, cols, rows * levels, inside),
        out_shape=(field_shape, out_shape),
        in_specs=[VMEM] * (7 + x_blocks),
        out_specs=(VMEM, HBM),
        scratch_shapes=[
            pltpu.VMEM((x_blocks, *block_shape), F32),
            pltpu.SemaphoreType.DMA((2 * x_blocks + len(inside),)),
        ],
        input_output_aliases={6: 0},
        name="edge",
        cost_estimate=takes(1.0),
        compiler_params=grant(6),
    )(table, second_got, glued, mask, near, done, field, *bands)
    return updated.reshape(cols, rows, levels, lanes)


def solution(mesh):
    split = P("gx", "gy", None, None)
    in_specs = (split, P("gx", "gy", None), P("gx", "gy", None), P(), P(), P())


    def run(tracers, weights, offsets, owner, codes):
        matrix = jnp.asarray(spread_matrix(tracers.shape[2]), BF16)
        body = jax.shard_map(
            on_device, mesh=mesh, in_specs=in_specs, out_specs=split, check_vma=False
        )
        return body(tracers, weights, offsets, owner, codes, matrix)

    return run
```

profile of v0, /device:TPU:0, one launch (start us, length us, event | category | flops | bytes accessed | tf_op | source)
XLA Modules:
  0.0 18.9 jit_solution(6026287953701084332)
XLA Ops:
  0.0 1.0 %pack.1 = (f32[144,128]{1,0:T(8,128)S(1)}, f32[96,128]{1,0:T(8,128)S(1)}, f32[3,128,128]{2,1,0:T(8,128)S(1)}) custom-call(f32[12,128,128]{2,1,0:T(8,128)} %bitcast.4), custom_call_target="tpu_custom_call" | custom-call | bytes 3000000 | tf_op jit(solution)/shard_map/pack/pallas_call | solution.py:439
  1.0 3.4 %collective-permute-start.6 = (f32[3,128,128]{2,1,0:T(8,128)S(1)}, f32[3,128,128]{2,1,0:T(8,128)S(1)}, u32[]{:S(2)}, u32[]{:S(2)}) collective-permute-start(f32[3,128,128]{2,1,0:T(8,128)S(1)} %get-tuple-element.48), channel_id=1, source_target_pairs={{0,28},{4,8},{8,4},{12,16},{16,12},{20,24},{24,20},{28,0},{1,29},{... | collective-permute-start | bytes 589832 | tf_op jit(solution)/shard_map/ppermute | solution.py:454
  4.5 0.1 load.2
  4.6 1.5 %load.3 = (s32[8,128]{1,0:T(8,128)S(1)}, f32[3,128,128]{2,1,0:T(8,128)S(1)}, f32[12,48,64]{2,1,0:T(8,128)S(1)}, s32[12,4,64]{2,1,0:T(4,128)S(1)}, bf16[104,512]{...) custom-call(s32[2,8]{1,0:T(2,128)} %owner_ref.3, ...), custom_call_target="tpu_custom_call", output_to_operand_aliasing={{0}: (7, {}), {1}: (8, {}), {2}: (9, {}), {3}: (10, {}), {4... | custom-call | bytes 1500000 | tf_op jit(solution)/shard_map/load/pallas_call | solution.py:473
  6.1 0.1 collective-permute-start.5
  6.1 0.7 %collective-permute-start = (f32[96,128]{1,0:T(8,128)S(1)}, f32[96,128]{1,0:T(8,128)S(1)}, u32[]{:S(2)}, u32[]{:S(2)}) collective-permute-start(f32[96,128]{1,0:T(8,128)S(1)} %get-tuple-element.30.after_ref.message_ref), channel_id=1, source_target_pairs={{0,28},{4,8},{8,4},{12,16},{16,12},{20,24},{24,20},{28,0},{1,29},{... | collective-permute-start | bytes 147464 | tf_op jit(solution)/shard_map/ppermute | solution.py:453
  6.8 4.3 %collective-permute-done.got_ref = f32[96,128]{1,0:T(8,128)S(1)} collective-permute-done((f32[96,128]{1,0:T(8,128)S(1)}, f32[96,128]{1,0:T(8,128)S(1)}, u32[]{:S(2)}, u32[]{:S(2)}) %collective-permute-start) | collective-permute-done | bytes 49184 | tf_op jit(solution)/shard_map/ppermute | solution.py:453
  11.1 0.1 collective-permute-start.1
  11.2 2.2 %collective-permute-start.3 = (f32[96,128]{1,0:T(8,128)S(1)}, f32[96,128]{1,0:T(8,128)S(1)}, u32[]{:S(2)}, u32[]{:S(2)}) collective-permute-start(f32[96,128]{1,0:T(8,128)S(1)} %get-tuple-element.40), channel_id=1, source_target_pairs={{0,1},{1,0},{2,3},{3,2},{4,5},{5,4},{6,7},{7,6},{8,9},{9,8},{10,11... | collective-permute-start | bytes 147464 | tf_op jit(solution)/shard_map/ppermute | solution.py:518
  13.4 0.0 collective-permute-done.1.other_ref
  13.4 0.1 rows.1.after_ref
  13.5 0.8 %collective-permute-start.2 = (f32[112,128]{1,0:T(8,128)S(1)}, f32[112,128]{1,0:T(8,128)S(1)}, u32[]{:S(2)}, u32[]{:S(2)}) collective-permute-start(f32[112,128]{1,0:T(8,128)S(1)} %rows.1.after_ref), channel_id=1, source_target_pairs={{0,16},{1,2},{2,1},{3,19},{4,20},{5,6},{6,5},{7,23},{8,24},{9,10},... | collective-permute-start | bytes 172040 | tf_op jit(solution)/shard_map/ppermute | solution.py:546
  14.3 0.4 %band.3.refs_0_ = bf16[8,128,256]{2,1,0:T(8,128)(2,1)S(1)} custom-call(f32[12,48,64]{2,1,0:T(8,128)S(1)} %get-tuple-element.41.weights_ref, s32[12,4,64]{2,1,0:T(4,128)S(1)} %get-tuple-element.42.offsets_ref, bf16[104,512]{1,0:T(8,128)(2,1)S(1)} %get-tuple-element.43.matrix_ref, f32[112,128]{1,0:T(8,128)S(1)} %rows.1.after_ref), custom_call_target="tpu_custom_call" | custom-call | bytes 1500000 | tf_op jit(solution)/shard_map/band/pallas_call | solution.py:495
  14.7 1.0 %collective-permute-done.3.first_ref = f32[96,128]{1,0:T(8,128)S(1)} collective-permute-done((f32[96,128]{1,0:T(8,128)S(1)}, f32[96,128]{1,0:T(8,128)S(1)}, u32[]{:S(2)}, u32[]{:S(2)}) %collective-permute-start.3) | collective-permute-done | bytes 49184 | tf_op jit(solution)/shard_map/ppermute | solution.py:518
  15.7 0.1 turn.1
  15.9 0.1 collective-permute-start.4
  15.9 0.4 %band.5.refs_2_ = bf16[8,128,256]{2,1,0:T(8,128)(2,1)S(1)} custom-call(f32[12,48,64]{2,1,0:T(8,128)S(1)} %get-tuple-element.41.weights_ref, s32[12,4,64]{2,1,0:T(4,128)S(1)} %get-tuple-element.42.offsets_ref, bf16[104,512]{1,0:T(8,128)(2,1)S(1)} %get-tuple-element.43.matrix_ref, f32[112,128]{1,0:T(8,128)S(1)} %rows.1.after_ref), custom_call_target="tpu_custom_call" | custom-call | bytes 1500000 | tf_op jit(solution)/shard_map/band/pallas_call | solution.py:495
  16.4 0.4 %band.4.refs_1_ = bf16[8,128,256]{2,1,0:T(8,128)(2,1)S(1)} custom-call(f32[12,48,64]{2,1,0:T(8,128)S(1)} %get-tuple-element.41.weights_ref, s32[12,4,64]{2,1,0:T(4,128)S(1)} %get-tuple-element.42.offsets_ref, bf16[104,512]{1,0:T(8,128)(2,1)S(1)} %get-tuple-element.43.matrix_ref, f32[112,128]{1,0:T(8,128)S(1)} %rows.1.after_ref), custom_call_target="tpu_custom_call" | custom-call | bytes 1500000 | tf_op jit(solution)/shard_map/band/pallas_call | solution.py:495
  16.8 0.0 collective-permute-done.6.outer_ref
  16.8 0.0 collective-permute-done.5.inner_ref
  16.9 0.4 %middle.1 = (f32[18,152,128]{2,1,0:T(8,128)S(1)}, f32[6,4,32,128]{3,2,1,0:T(8,128)S(1)}) custom-call(f32[3,128,128]{2,1,0:T(8,128)S(1)} %collective-permute-done.5.inner_ref, f32[3,128,128]{2,1,0:T(8,128)S(1)} %collective-permute-done.6.outer_ref, f32[112,128]{1,0:T(8,128)S(1)} %rows.1.after_ref, ...), custom_call_target="tpu_custom_call", output_to_operand_aliasing={{0}: (3, {})} | custom-call | bytes 2100000 | tf_op jit(solution)/shard_map/middle/pallas_call | solution.py:572
  17.3 0.3 %near.1 = (f32[18,152,128]{2,1,0:T(8,128)S(1)}, f32[3,4,32,128]{3,2,1,0:T(8,128)S(1)}) custom-call(f32[96,128]{1,0:T(8,128)S(1)} %collective-permute-done.3.first_ref, f32[24,128]{1,0:T(8,128)S(1)} %collective-permute-done.4.corner_ref, f32[18,152,128]{2,1,0:T(8,128)S(1)} %get-tuple-element.50.field_in, ...), custom_call_target="tpu_custom_call", output_to_operand_aliasing={{0}: (2, {})} | custom-call | bytes 1500000 | tf_op jit(solution)/shard_map/near/pallas_call | solution.py:574
  17.6 0.1 collective-permute-done.2.second_ref
  17.7 1.1 %edge.1 = (f32[18,152,128]{2,1,0:T(8,128)S(1)}, f32[12,128,128]{2,1,0:T(8,128)}) custom-call(s32[8,128]{1,0:T(8,128)S(1)} %get-tuple-element.37.after_ref.table_ref.refs_2_, f32[112,128]{1,0:T(8,128)S(1)} %collective-permute-done.2.second_ref, f32[112,128]{1,0:T(8,128)S(1)} %get-tuple-element.44.glued_ref, ...), custom_call_target="tpu_custom_call", output_to_operand_aliasing={{0}: (6, {})} | custom-call | bytes 3000000 | tf_op jit(solution)/shard_map/edge/pallas_call | solution.py:584
  (3 shorter events, 0.0 us)
Async XLA Ops:
  1.0 15.8 %collective-permute-start.6 = (f32[3,128,128]{2,1,0:T(8,128)S(1)}, f32[3,128,128]{2,1,0:T(8,128)S(1)}, u32[]{:S(2)}, u32[]{:S(2)}) collective-permute-start(f32[3,128,128]{2,1,0:T(8,128)S(1)} %get-tuple-element.48), channel_id=1, source_target_pairs={{0,28},{4,8},{8,4},{12,16},{16,12},{20,24},{24,20},{28,0},{1,29},{... | collective-permute-start | bytes 589832 | tf_op jit(solution)/shard_map/ppermute | solution.py:454
  6.1 10.8 %collective-permute-start.5 = (f32[3,128,128]{2,1,0:T(8,128)S(1)}, f32[3,128,128]{2,1,0:T(8,128)S(1)}, u32[]{:S(2)}, u32[]{:S(2)}) collective-permute-start(f32[3,128,128]{2,1,0:T(8,128)S(1)} %get-tuple-element.47), channel_id=1, source_target_pairs={{0,4},{4,0},{8,12},{12,8},{16,20},{20,16},{24,28},{28,24},{1,5},{5... | collective-permute-start | bytes 589832 | tf_op jit(solution)/shard_map/ppermute | solution.py:519
  6.1 5.0 %collective-permute-start = (f32[96,128]{1,0:T(8,128)S(1)}, f32[96,128]{1,0:T(8,128)S(1)}, u32[]{:S(2)}, u32[]{:S(2)}) collective-permute-start(f32[96,128]{1,0:T(8,128)S(1)} %get-tuple-element.30.after_ref.message_ref), channel_id=1, source_target_pairs={{0,28},{4,8},{8,4},{12,16},{16,12},{20,24},{24,20},{28,0},{1,29},{... | collective-permute-start | bytes 147464 | tf_op jit(solution)/shard_map/ppermute | solution.py:453
  11.1 2.3 %collective-permute-start.1 = (f32[144,128]{1,0:T(8,128)S(1)}, f32[144,128]{1,0:T(8,128)S(1)}, u32[]{:S(2)}, u32[]{:S(2)}) collective-permute-start(f32[144,128]{1,0:T(8,128)S(1)} %get-tuple-element.39.after_ref), channel_id=1, source_target_pairs={{0,4},{4,0},{8,12},{12,8},{16,20},{20,16},{24,28},{28,24},{1,5},{5... | collective-permute-start | bytes 221192 | tf_op jit(solution)/shard_map/ppermute | solution.py:517
  11.2 4.5 %collective-permute-start.3 = (f32[96,128]{1,0:T(8,128)S(1)}, f32[96,128]{1,0:T(8,128)S(1)}, u32[]{:S(2)}, u32[]{:S(2)}) collective-permute-start(f32[96,128]{1,0:T(8,128)S(1)} %get-tuple-element.40), channel_id=1, source_target_pairs={{0,1},{1,0},{2,3},{3,2},{4,5},{5,4},{6,7},{7,6},{8,9},{9,8},{10,11... | collective-permute-start | bytes 147464 | tf_op jit(solution)/shard_map/ppermute | solution.py:518
  13.5 4.2 %collective-permute-start.2 = (f32[112,128]{1,0:T(8,128)S(1)}, f32[112,128]{1,0:T(8,128)S(1)}, u32[]{:S(2)}, u32[]{:S(2)}) collective-permute-start(f32[112,128]{1,0:T(8,128)S(1)} %rows.1.after_ref), channel_id=1, source_target_pairs={{0,16},{1,2},{2,1},{3,19},{4,20},{5,6},{6,5},{7,23},{8,24},{9,10},... | collective-permute-start | bytes 172040 | tf_op jit(solution)/shard_map/ppermute | solution.py:546
  15.9 1.4 %collective-permute-start.4 = (f32[24,128]{1,0:T(8,128)S(1)}, f32[24,128]{1,0:T(8,128)S(1)}, u32[]{:S(2)}, u32[]{:S(2)}) collective-permute-start(f32[24,128]{1,0:T(8,128)S(1)} %get-tuple-element.46), channel_id=1, source_target_pairs={{0,4},{4,0},{8,12},{12,8},{16,20},{20,16},{24,28},{28,24},{1,5},{5... | collective-permute-start | bytes 36872 | tf_op jit(solution)/shard_map/ppermute | solution.py:559
where the time goes:
time: 19 us; the launch traced here: 18.9 us
  starting transfers between devices  7.31 us (38%)
  Pallas kernels  6.06 us (32%)
  waiting for transfers between devices  5.38 us (28%)
    ppermute x1, waiting for transfers between devices, on_device(): got = lax.ppermute(message, 'gx', across)  4.25 us
    ppermute x1, starting transfers between devices, on_device(): outer_got = lax.ppermute(outer, 'gx', across)  3.43 us
    ppermute x1, starting transfers between devices, on_device(): first_got = lax.ppermute(first, axes, first_swap)  2.19 us
    pallas_call x2, Pallas kernels, load(): pl.pallas_call(functools.partial(load_kernel, count, ends, held, turns),...  1.57 us
    pallas_call x3, Pallas kernels, band_of(): pl.pallas_call(functools.partial(band_kernel, levels, rows, block), out_s...  1.33 us
    pallas_call x1, Pallas kernels, on_device(): pl.pallas_call(functools.partial(edge_kernel, levels, cols, rows * levels...  1.14 us
    pallas_call x1, Pallas kernels, on_device(): pl.pallas_call(functools.partial(pack_kernel, ends), out_shape=(shaped(2...  1.04 us
    ppermute x1, waiting for transfers between devices, on_device(): first_got = lax.ppermute(first, axes, first_swap)  0.99 us
  transfers between devices with their start and end apart: 7, of which 3 were waited for; matrix products, arithmetic and copies ran while one was open for 0% of the time, Pallas kernels for 21%

commit v1 on v0

--- a/solution.py
+++ b/solution.py
@@ -364,14 +364,13 @@
     copies = []
     ready = [(done_ref.at[at], x, y) for at, (x, y) in enumerate(done)]
     ready += [(near_ref.at[x], x, last - y) for x, y in blocks]
-    for source, x, y in ready:
-        copies.append(put_block(source, out_ref, sems.at[len(copies)], x, y))
 
     def put(at, x, y):
         copies.append(put_block(stage_ref.at[at], out_ref, sems.at[len(copies)], x, y))
 
     width, lead = HALO * levels, LEAD * levels
     wide = cols + 2 * HALO
+    facing = jnp.where(up, lead - width, lead + rows)
     code = table_ref[2:3, 0:1][0, 0]
     mirrored, flipped = code % 2 == 1, code // 2 % 2 == 1
     for u in range(wide):
@@ -380,9 +379,11 @@
         come = jnp.where(mirrored, second_ref[back], second_ref[to])
         come = jnp.where(flipped, turn_rows(come, levels), come)
         strip = jnp.where(mask_ref[to] > 0, glued_ref[to], come)
-        for at, mine in ((lead - width, up), (lead + rows, jnp.logical_not(up))):
-            old = field_ref[u, at : at + width]
-            field_ref[u, at : at + width] = jnp.where(mine, strip, old)
+        field_ref[u, pl.ds(facing, width)] = strip
+
+    for source, x, y in ready:
+        copies.append(put_block(source, out_ref, sems.at[len(copies)], x, y))
+
     remap_blocks(field_ref, bands, stage_ref, levels, blocks, put)
     for copy in copies:
         copy.wait()
@@ -550,12 +551,12 @@
     turned, glued, mask = pl.pallas_call(
         functools.partial(turn_kernel, levels, cols, width, count, ends, run),
         out_shape=(shaped(eights(width * HALO), lanes), shaped(z_rows, lanes), shaped(z_rows, lanes)),
-        in_specs=[VMEM] + [ANY] * len(bands[:1]) + [VMEM] * 2,
+        in_specs=[VMEM] + [ANY] * len(bands[:2]) + [VMEM] * 2,
         out_specs=(VMEM, VMEM, VMEM),
         name="turn",
         compiler_params=grant(2),
         cost_estimate=takes(0.1),
-    )(first_got, *bands[:1], ring, table)
+    )(first_got, *bands[:2], ring, table)
     turned_got = lax.ppermute(turned, "gx", partner)
     inside = [(x, y) for y in range(1, y_blocks - 1) for x in range(x_blocks)]
     block_shape = (BLOCK_X, BLOCK_Y * levels, lanes)

time: 19 us -> 19.1 us (level)
    ppermute x1, waiting for transfers between devices: 0.99 us -> 0.54 us  [on_device(): first_got = lax.ppermute(first, axes, first_swap)]
    ppermute x1, waiting for transfers between devices: 0.01 us -> 0.26 us  [on_device(): turned_got = lax.ppermute(turned, 'gx', partner)]
    ppermute x1, waiting for transfers between devices: 0.13 us -> 0.34 us  [on_device(): second_got = lax.ppermute(second, axes, second_swap)]
  transfers between devices with their start and end apart: 7 -> 7, of which waited for: 3 -> 4; matrix products, arithmetic and copies ran while one was open for 0% -> 0% of each run, Pallas kernels for 21% -> 21%
where the time goes in v1:
time: 19.1 us; the launch traced here: 18.9 us
  starting transfers between devices  7.31 us (38%)
  Pallas kernels  6.06 us (32%)
  waiting for transfers between devices  5.4 us (28%)
    ppermute x1, waiting for transfers between devices, on_device(): got = lax.ppermute(message, 'gx', across)  4.25 us
    ppermute x1, starting transfers between devices, on_device(): outer_got = lax.ppermute(outer, 'gx', across)  3.43 us
    ppermute x1, starting transfers between devices, on_device(): first_got = lax.ppermute(first, axes, first_swap)  2.19 us
    pallas_call x2, Pallas kernels, load(): pl.pallas_call(functools.partial(load_kernel, count, ends, held, turns),...  1.57 us
    pallas_call x3, Pallas kernels, band_of(): pl.pallas_call(functools.partial(band_kernel, levels, rows, block), out_s...  1.33 us
    pallas_call x1, Pallas kernels, on_device(): pl.pallas_call(functools.partial(edge_kernel, levels, cols, rows * levels...  1.15 us
    pallas_call x1, Pallas kernels, on_device(): pl.pallas_call(functools.partial(pack_kernel, ends), out_shape=(shaped(2...  1.04 us
    ppermute x1, starting transfers between devices, on_device(): second_got = lax.ppermute(second, axes, second_swap)  0.78 us
  transfers between devices with their start and end apart: 7, of which 4 were waited for; matrix products, arithmetic and copies ran while one was open for 0% of the time, Pallas kernels for 21%

profile of v1, /device:TPU:0, one launch (start us, length us, event | category | flops | bytes accessed | tf_op | source)
XLA Modules:
  0.0 18.9 jit_solution(17791676874108306505)
XLA Ops:
  0.0 1.0 %pack.1 = (f32[144,128]{1,0:T(8,128)S(1)}, f32[96,128]{1,0:T(8,128)S(1)}, f32[3,128,128]{2,1,0:T(8,128)S(1)}) custom-call(f32[12,128,128]{2,1,0:T(8,128)} %bitcast.4), custom_call_target="tpu_custom_call" | custom-call | bytes 3000000 | tf_op jit(solution)/shard_map/pack/pallas_call | solution.py:440
  1.0 3.4 %collective-permute-start.6 = (f32[3,128,128]{2,1,0:T(8,128)S(1)}, f32[3,128,128]{2,1,0:T(8,128)S(1)}, u32[]{:S(2)}, u32[]{:S(2)}) collective-permute-start(f32[3,128,128]{2,1,0:T(8,128)S(1)} %get-tuple-element.48), channel_id=1, source_target_pairs={{0,28},{4,8},{8,4},{12,16},{16,12},{20,24},{24,20},{28,0},{1,29},{... | collective-permute-start | bytes 589832 | tf_op jit(solution)/shard_map/ppermute | solution.py:455
  4.5 0.1 load.2
  4.6 1.5 %load.3 = (s32[8,128]{1,0:T(8,128)S(1)}, f32[3,128,128]{2,1,0:T(8,128)S(1)}, f32[12,48,64]{2,1,0:T(8,128)S(1)}, s32[12,4,64]{2,1,0:T(4,128)S(1)}, bf16[104,512]{...) custom-call(s32[2,8]{1,0:T(2,128)} %owner_ref.3, ...), custom_call_target="tpu_custom_call", output_to_operand_aliasing={{0}: (7, {}), {1}: (8, {}), {2}: (9, {}), {3}: (10, {}), {4... | custom-call | bytes 1500000 | tf_op jit(solution)/shard_map/load/pallas_call | solution.py:474
  6.1 0.1 collective-permute-start.5
  6.1 0.7 %collective-permute-start = (f32[96,128]{1,0:T(8,128)S(1)}, f32[96,128]{1,0:T(8,128)S(1)}, u32[]{:S(2)}, u32[]{:S(2)}) collective-permute-start(f32[96,128]{1,0:T(8,128)S(1)} %get-tuple-element.30.after_ref.message_ref), channel_id=1, source_target_pairs={{0,28},{4,8},{8,4},{12,16},{16,12},{20,24},{24,20},{28,0},{1,29},{... | collective-permute-start | bytes 147464 | tf_op jit(solution)/shard_map/ppermute | solution.py:454
  6.8 4.3 %collective-permute-done.got_ref = f32[96,128]{1,0:T(8,128)S(1)} collective-permute-done((f32[96,128]{1,0:T(8,128)S(1)}, f32[96,128]{1,0:T(8,128)S(1)}, u32[]{:S(2)}, u32[]{:S(2)}) %collective-permute-start) | collective-permute-done | bytes 49184 | tf_op jit(solution)/shard_map/ppermute | solution.py:454
  11.1 0.1 collective-permute-start.1
  11.2 2.2 %collective-permute-start.3 = (f32[96,128]{1,0:T(8,128)S(1)}, f32[96,128]{1,0:T(8,128)S(1)}, u32[]{:S(2)}, u32[]{:S(2)}) collective-permute-start(f32[96,128]{1,0:T(8,128)S(1)} %get-tuple-element.40), channel_id=1, source_target_pairs={{0,1},{1,0},{2,3},{3,2},{4,5},{5,4},{6,7},{7,6},{8,9},{9,8},{10,11... | collective-permute-start | bytes 147464 | tf_op jit(solution)/shard_map/ppermute | solution.py:519
  13.4 0.0 collective-permute-done.1.other_ref
  13.4 0.1 rows.1.after_ref
  13.5 0.8 %collective-permute-start.2 = (f32[112,128]{1,0:T(8,128)S(1)}, f32[112,128]{1,0:T(8,128)S(1)}, u32[]{:S(2)}, u32[]{:S(2)}) collective-permute-start(f32[112,128]{1,0:T(8,128)S(1)} %rows.1.after_ref), channel_id=1, source_target_pairs={{0,16},{1,2},{2,1},{3,19},{4,20},{5,6},{6,5},{7,23},{8,24},{9,10},... | collective-permute-start | bytes 172040 | tf_op jit(solution)/shard_map/ppermute | solution.py:547
  14.3 0.4 %band.4.refs_1_ = bf16[8,128,256]{2,1,0:T(8,128)(2,1)S(1)} custom-call(f32[12,48,64]{2,1,0:T(8,128)S(1)} %get-tuple-element.41.weights_ref, s32[12,4,64]{2,1,0:T(4,128)S(1)} %get-tuple-element.42.offsets_ref, bf16[104,512]{1,0:T(8,128)(2,1)S(1)} %get-tuple-element.43.matrix_ref, f32[112,128]{1,0:T(8,128)S(1)} %rows.1.after_ref), custom_call_target="tpu_custom_call" | custom-call | bytes 1500000 | tf_op jit(solution)/shard_map/band/pallas_call | solution.py:496
  14.7 0.4 %band.3.refs_0_ = bf16[8,128,256]{2,1,0:T(8,128)(2,1)S(1)} custom-call(f32[12,48,64]{2,1,0:T(8,128)S(1)} %get-tuple-element.41.weights_ref, s32[12,4,64]{2,1,0:T(4,128)S(1)} %get-tuple-element.42.offsets_ref, bf16[104,512]{1,0:T(8,128)(2,1)S(1)} %get-tuple-element.43.matrix_ref, f32[112,128]{1,0:T(8,128)S(1)} %rows.1.after_ref), custom_call_target="tpu_custom_call" | custom-call | bytes 1500000 | tf_op jit(solution)/shard_map/band/pallas_call | solution.py:496
  15.2 0.5 %collective-permute-done.3.first_ref = f32[96,128]{1,0:T(8,128)S(1)} collective-permute-done((f32[96,128]{1,0:T(8,128)S(1)}, f32[96,128]{1,0:T(8,128)S(1)}, u32[]{:S(2)}, u32[]{:S(2)}) %collective-permute-start.3) | collective-permute-done | bytes 49184 | tf_op jit(solution)/shard_map/ppermute | solution.py:519
  15.7 0.1 turn.1
  15.9 0.1 collective-permute-start.4
  15.9 0.4 %band.5.refs_2_ = bf16[8,128,256]{2,1,0:T(8,128)(2,1)S(1)} custom-call(f32[12,48,64]{2,1,0:T(8,128)S(1)} %get-tuple-element.41.weights_ref, s32[12,4,64]{2,1,0:T(4,128)S(1)} %get-tuple-element.42.offsets_ref, bf16[104,512]{1,0:T(8,128)(2,1)S(1)} %get-tuple-element.43.matrix_ref, f32[112,128]{1,0:T(8,128)S(1)} %rows.1.after_ref), custom_call_target="tpu_custom_call" | custom-call | bytes 1500000 | tf_op jit(solution)/shard_map/band/pallas_call | solution.py:496
  16.4 0.0 collective-permute-done.6.outer_ref
  16.4 0.4 %middle.1 = (f32[18,152,128]{2,1,0:T(8,128)S(1)}, f32[6,4,32,128]{3,2,1,0:T(8,128)S(1)}) custom-call(f32[3,128,128]{2,1,0:T(8,128)S(1)} %collective-permute-done.5.inner_ref, f32[3,128,128]{2,1,0:T(8,128)S(1)} %collective-permute-done.6.outer_ref, f32[112,128]{1,0:T(8,128)S(1)} %rows.1.after_ref, ...), custom_call_target="tpu_custom_call", output_to_operand_aliasing={{0}: (3, {})} | custom-call | bytes 2100000 | tf_op jit(solution)/shard_map/middle/pallas_call | solution.py:573
  16.8 0.3 %collective-permute-done.4.corner_ref = f32[24,128]{1,0:T(8,128)S(1)} collective-permute-done((f32[24,128]{1,0:T(8,128)S(1)}, f32[24,128]{1,0:T(8,128)S(1)}, u32[]{:S(2)}, u32[]{:S(2)}) %collective-permute-start.4) | collective-permute-done | bytes 12320 | tf_op jit(solution)/shard_map/ppermute | solution.py:560
  17.1 0.3 %near.1 = (f32[18,152,128]{2,1,0:T(8,128)S(1)}, f32[3,4,32,128]{3,2,1,0:T(8,128)S(1)}) custom-call(f32[96,128]{1,0:T(8,128)S(1)} %collective-permute-done.3.first_ref, f32[24,128]{1,0:T(8,128)S(1)} %collective-permute-done.4.corner_ref, f32[18,152,128]{2,1,0:T(8,128)S(1)} %get-tuple-element.50.field_in, ...), custom_call_target="tpu_custom_call", output_to_operand_aliasing={{0}: (2, {})} | custom-call | bytes 1500000 | tf_op jit(solution)/shard_map/near/pallas_call | solution.py:575
  17.4 0.3 %collective-permute-done.2.second_ref = f32[112,128]{1,0:T(8,128)S(1)} collective-permute-done((f32[112,128]{1,0:T(8,128)S(1)}, f32[112,128]{1,0:T(8,128)S(1)}, u32[]{:S(2)}, u32[]{:S(2)}) %collective-permute-start.2) | collective-permute-done | bytes 57376 | tf_op jit(solution)/shard_map/ppermute | solution.py:547
  17.7 1.1 %edge.1 = (f32[18,152,128]{2,1,0:T(8,128)S(1)}, f32[12,128,128]{2,1,0:T(8,128)}) custom-call(s32[8,128]{1,0:T(8,128)S(1)} %get-tuple-element.37.after_ref.table_ref.refs_3_, f32[112,128]{1,0:T(8,128)S(1)} %collective-permute-done.2.second_ref, f32[112,128]{1,0:T(8,128)S(1)} %get-tuple-element.44.glued_ref, ...), custom_call_target="tpu_custom_call", output_to_operand_aliasing={{0}: (6, {})} | custom-call | bytes 3000000 | tf_op jit(solution)/shard_map/edge/pallas_call | solution.py:585
  (3 shorter events, 0.0 us)
Async XLA Ops:
  1.0 15.3 %collective-permute-start.6 = (f32[3,128,128]{2,1,0:T(8,128)S(1)}, f32[3,128,128]{2,1,0:T(8,128)S(1)}, u32[]{:S(2)}, u32[]{:S(2)}) collective-permute-start(f32[3,128,128]{2,1,0:T(8,128)S(1)} %get-tuple-element.48), channel_id=1, source_target_pairs={{0,28},{4,8},{8,4},{12,16},{16,12},{20,24},{24,20},{28,0},{1,29},{... | collective-permute-start | bytes 589832 | tf_op jit(solution)/shard_map/ppermute | solution.py:455
  6.1 10.3 %collective-permute-start.5 = (f32[3,128,128]{2,1,0:T(8,128)S(1)}, f32[3,128,128]{2,1,0:T(8,128)S(1)}, u32[]{:S(2)}, u32[]{:S(2)}) collective-permute-start(f32[3,128,128]{2,1,0:T(8,128)S(1)} %get-tuple-element.47), channel_id=1, source_target_pairs={{0,4},{4,0},{8,12},{12,8},{16,20},{20,16},{24,28},{28,24},{1,5},{5... | collective-permute-start | bytes 589832 | tf_op jit(solution)/shard_map/ppermute | solution.py:520
  6.1 5.0 %collective-permute-start = (f32[96,128]{1,0:T(8,128)S(1)}, f32[96,128]{1,0:T(8,128)S(1)}, u32[]{:S(2)}, u32[]{:S(2)}) collective-permute-start(f32[96,128]{1,0:T(8,128)S(1)} %get-tuple-element.30.after_ref.message_ref), channel_id=1, source_target_pairs={{0,28},{4,8},{8,4},{12,16},{16,12},{20,24},{24,20},{28,0},{1,29},{... | collective-permute-start | bytes 147464 | tf_op jit(solution)/shard_map/ppermute | solution.py:454
  11.1 2.3 %collective-permute-start.1 = (f32[144,128]{1,0:T(8,128)S(1)}, f32[144,128]{1,0:T(8,128)S(1)}, u32[]{:S(2)}, u32[]{:S(2)}) collective-permute-start(f32[144,128]{1,0:T(8,128)S(1)} %get-tuple-element.39.after_ref), channel_id=1, source_target_pairs={{0,4},{4,0},{8,12},{12,8},{16,20},{20,16},{24,28},{28,24},{1,5},{5... | collective-permute-start | bytes 221192 | tf_op jit(solution)/shard_map/ppermute | solution.py:518
  11.2 4.5 %collective-permute-start.3 = (f32[96,128]{1,0:T(8,128)S(1)}, f32[96,128]{1,0:T(8,128)S(1)}, u32[]{:S(2)}, u32[]{:S(2)}) collective-permute-start(f32[96,128]{1,0:T(8,128)S(1)} %get-tuple-element.40), channel_id=1, source_target_pairs={{0,1},{1,0},{2,3},{3,2},{4,5},{5,4},{6,7},{7,6},{8,9},{9,8},{10,11... | collective-permute-start | bytes 147464 | tf_op jit(solution)/shard_map/ppermute | solution.py:519
  13.5 4.2 %collective-permute-start.2 = (f32[112,128]{1,0:T(8,128)S(1)}, f32[112,128]{1,0:T(8,128)S(1)}, u32[]{:S(2)}, u32[]{:S(2)}) collective-permute-start(f32[112,128]{1,0:T(8,128)S(1)} %rows.1.after_ref), channel_id=1, source_target_pairs={{0,16},{1,2},{2,1},{3,19},{4,20},{5,6},{6,5},{7,23},{8,24},{9,10},... | collective-permute-start | bytes 172040 | tf_op jit(solution)/shard_map/ppermute | solution.py:547
  15.9 1.2 %collective-permute-start.4 = (f32[24,128]{1,0:T(8,128)S(1)}, f32[24,128]{1,0:T(8,128)S(1)}, u32[]{:S(2)}, u32[]{:S(2)}) collective-permute-start(f32[24,128]{1,0:T(8,128)S(1)} %get-tuple-element.46), channel_id=1, source_target_pairs={{0,4},{4,0},{8,12},{12,8},{16,20},{20,16},{24,28},{28,24},{1,5},{5... | collective-permute-start | bytes 36872 | tf_op jit(solution)/shard_map/ppermute | solution.py:560
